TPU v7x, 32 devices: a whole 2x2x4 slice. The times are simulated.
32 devices in a mesh: freq: 8 (over y, x, core), rcv: 4 (over z).
Axes of the slice: x: 2, y: 2, z: 4, core: 2. Of those that a mesh axis runs over, the one named last changes fastest.
Arguments:
- green_freq: float32 [2, 8, 2304, 2304], P(None, 'freq', 'rcv'), may hold values from -6 to 6
- data_matrix: float32 [2, 8, 2304, 2304], P(None, 'freq', 'rcv'), may hold values from -0.09375 to 0.09375
- shot_panels: float32 [2, 8, 2304, 256], P(None, 'freq', 'rcv'), may hold values from -6 to 6
- wavelet: float32 [2, 8], P(None, 'freq'), may hold values from -1.5 to 1.5
- sources: int32 [256], replicated, may hold values from 0 to 2303, as said below
- support: int32 [8, 2304], replicated, may hold values 0 or 1
- threshold: float32 [1], replicated, may hold values from 3 to 7
Outputs:
- green_next: float32 [2, 8, 2304, 2304], P(None, 'freq', 'rcv')
- residual: float32 [2, 8, 2304, 256], P(None, 'freq', 'rcv')
Inputs may be any that keep to these rules, and one draw needn't show every extreme that they name: `sources`: 256 distinct source positions. `support`: a 0/1 mask over time samples and source positions.
All inputs are finite; a program needn't handle non-finite values.
Results may differ from a plain program's by a relative error of at most 0.00013.
Values sent between devices are 32-bit elements; how exact they have to be, the bound alone decides.
A program may use at most 128 MiB of HBM per device.

v0:
```python
import math

import jax
import jax.numpy as jnp
from jax import lax
from jax.sharding import PartitionSpec as P

HIGHEST = lax.Precision.HIGHEST


def complex_product(left_pair, right_pair, pattern):
    left_real, left_imag = left_pair
    right_real, right_imag = right_pair
    real_part = jnp.einsum(pattern, left_real, right_real, precision=HIGHEST) - jnp.einsum(
        pattern, left_imag, right_imag, precision=HIGHEST
    )
    imag_part = jnp.einsum(pattern, left_real, right_imag, precision=HIGHEST) + jnp.einsum(
        pattern, left_imag, right_real, precision=HIGHEST
    )
    return (real_part, imag_part)


def conj_product(left_pair, right_pair, pattern):
    left_real, left_imag = left_pair
    right_real, right_imag = right_pair
    real_part = jnp.einsum(pattern, left_real, right_real, precision=HIGHEST) + jnp.einsum(
        pattern, left_imag, right_imag, precision=HIGHEST
    )
    imag_part = jnp.einsum(pattern, left_real, right_imag, precision=HIGHEST) - jnp.einsum(
        pattern, left_imag, right_real, precision=HIGHEST
    )
    return (real_part, imag_part)


def shrink_spectra(spectra, keep, shrink_level):
    n_freq = spectra.shape[1]
    grid = jnp.arange(n_freq, dtype=jnp.int32)
    phase = grid[:, None] * grid[None, :] % n_freq
    angle = phase.astype(jnp.float32) * (2.0 * math.pi / n_freq)
    cos_table = jnp.cos(angle)
    sin_table = jnp.sin(angle)
    pattern = "tf,f...->t..."
    time_real = jnp.einsum(pattern, cos_table, spectra[0], precision=HIGHEST) - jnp.einsum(
        pattern, sin_table, spectra[1], precision=HIGHEST
    )
    time_imag = jnp.einsum(pattern, sin_table, spectra[0], precision=HIGHEST) + jnp.einsum(
        pattern, cos_table, spectra[1], precision=HIGHEST
    )
    magnitude = jnp.sqrt(time_real * time_real + time_imag * time_imag)
    factor = (
        jnp.maximum(magnitude - shrink_level, 0.0) / jnp.maximum(magnitude, shrink_level) * keep
    )
    kept_real = factor * time_real
    kept_imag = factor * time_imag
    back_real = (
        jnp.einsum(pattern, cos_table, kept_real, precision=HIGHEST)
        + jnp.einsum(pattern, sin_table, kept_imag, precision=HIGHEST)
    ) / n_freq
    back_imag = (
        jnp.einsum(pattern, cos_table, kept_imag, precision=HIGHEST)
        - jnp.einsum(pattern, sin_table, kept_real, precision=HIGHEST)
    ) / n_freq
    return jnp.stack([back_real, back_imag])


def on_device(green_freq, data_matrix, shot_panels, wavelet, sources, support, threshold):
    data_pair = (data_matrix[0], data_matrix[1])
    picked = jnp.take(green_freq, sources, axis=3)
    wave_real = wavelet[0][:, None, None]
    wave_imag = wavelet[1][:, None, None]
    rows_here = green_freq.shape[2]
    shard_piece = lax.all_gather(picked, "rcv", axis=2, tiled=True)
    block_real = data_matrix[0]
    block_imag = data_matrix[1]
    real_part, imag_part = complex_product(
        (block_real, block_imag), (shard_piece[0], shard_piece[1]), "frk,fkc->frc"
    )
    multiple = jnp.stack([real_part, imag_part])
    resid_real = shot_panels[0] - (wave_real * picked[0] - wave_imag * picked[1] - multiple[0])
    resid_imag = shot_panels[1] - (wave_real * picked[1] + wave_imag * picked[0] - multiple[1])
    residual = jnp.stack([resid_real, resid_imag])
    local_real = wave_real * resid_real + wave_imag * resid_imag
    local_imag = wave_real * resid_imag - wave_imag * resid_real
    adj_real, adj_imag = conj_product(data_pair, (resid_real, resid_imag), "frk,frc->kfc")
    summed_terms = -jnp.stack([adj_real, adj_imag], axis=1)
    own_rows = jnp.transpose(jnp.stack([local_real, local_imag]), (2, 0, 1, 3))
    row_offset = lax.axis_index("rcv") * rows_here
    summed_terms = summed_terms + lax.dynamic_update_slice_in_dim(
        jnp.zeros_like(summed_terms), own_rows, row_offset, 0
    )
    summed_all = lax.psum(summed_terms, "rcv")
    mine = lax.dynamic_slice_in_dim(summed_all, row_offset, rows_here, 0)
    direction = jnp.transpose(mine, (1, 2, 0, 3))
    push_real, push_imag = complex_product(
        data_pair, (summed_all[:, 0], summed_all[:, 1]), "frk,kfc->frc"
    )
    pushed = jnp.stack([push_real, push_imag])
    image_real = wave_real * direction[0] - wave_imag * direction[1] - pushed[0]
    image_imag = wave_real * direction[1] + wave_imag * direction[0] - pushed[1]
    norm_dir = jnp.sum(direction * direction)
    norm_img = jnp.sum(image_real * image_real + image_imag * image_imag)
    totals = lax.psum((norm_dir, norm_img), ("freq", "rcv"))
    step_size = totals[0] / totals[1]
    updated = green_freq.at[:, :, :, sources].add(step_size * direction)
    keep_all = support.astype(jnp.float32)
    gathered = lax.all_to_all(updated, "freq", split_axis=2, concat_axis=1, tiled=True)
    shrunk = shrink_spectra(gathered, keep_all[:, None, :], threshold[0])
    green_next = lax.all_to_all(shrunk, "freq", split_axis=1, concat_axis=2, tiled=True)
    return (green_next, residual)


def solution(mesh):
    in_specs = (
        P(None, "freq", "rcv", None),
        P(None, "freq", "rcv", None),
        P(None, "freq", "rcv", None),
        P(None, "freq"),
        P(),
        P(),
        P(),
    )
    out_specs = (P(None, "freq", "rcv", None), P(None, "freq", "rcv", None))
    return jax.shard_map(
        on_device, mesh=mesh, in_specs=in_specs, out_specs=out_specs, check_vma=False
    )
```

profile of v0, /device:TPU:1, one launch (start us, length us, event | category | flops | bytes accessed | tf_op | source)
XLA Modules:
  0.0 847.7 jit_solution(611839117997585425)
XLA Ops:
  8.6 19.2 %copy.30 = f32[2,1,576,2304]{2,0,3,1:T(2,128)} copy(f32[2,1,576,2304]{3,2,1,0:T(8,128)} %param.7) | data formatting | bytes 21233664 | tf_op args[0]
  27.8 6.5 gather_fusion
  37.8 90.5 %all-gather.2.cloned.1.call-done = f32[2,1,2304,256]{3,2,1,0:T(8,128)} async-done(((f32[2,1,576,256]{3,2,1,0:T(8,128)}), f32[2,1,2304,256]{3,2,1,0:T(8,128)}) %all-gather.2.cloned.1.call-update) | async-done | bytes 4718608 | tf_op jit(solution)/shard_map/all_gather | solution.py:72
  128.3 7.5 fusion.8
  135.8 9.7 %fusion.101 = f32[576,256]{1,0:T(8,128)S(1)} fusion(f32[256,576]{0,1:T(8,128)S(1)} %fusion.8, f32[2,1,576,2304]{3,2,1,0:T(8,128)} %param.8, f32[2,1,2304,256]{3,2,1,0:T(8,128)} %all-gather.2.cloned.1.call-done, f32[2,1,576,256]{3,2,1,0:T(8,128)} %param.9, f32[2,1,576,256]{3,2,1,0:T(8,128)S(1)} %copy-done.2, f32[]{:T(128)} %bitcast.6, f32[]{:T(128)} %bitcast.3), kind=kOutput, calls=%fused_computation.76 | convolution fusion | flops 4077748224 | bytes 10617856 | tf_op jit(solution)/shard_map/frk,fkc->frc/dot_general | solution.py:17
  145.5 11.9 %fusion.6 = f32[256,2304]{0,1:T(8,128)S(1)} fusion(f32[576,256]{1,0:T(8,128)S(1)} %fusion.101, f32[2,1,576,2304]{3,2,1,0:T(8,128)} %param.8), kind=kOutput, calls=%fused_computation.9 | convolution fusion | flops 4076863488 | bytes 8257536 | tf_op jit(solution)/shard_map/frk,frc->kfc/dot_general | solution.py:26
  161.9 5.7 fusion.98
  167.6 9.6 %fusion.4 = f32[256,2304]{0,1:T(8,128)S(1)} fusion(f32[576,256]{1,0:T(8,128)S(1)} %fusion.98, f32[2,1,576,2304]{3,2,1,0:T(8,128)S(1)} %bitcast.238), kind=kOutput, calls=%fused_computation.7 | convolution fusion | flops 4076863488 | bytes 8257536 | tf_op jit(solution)/shard_map/frk,frc->kfc/dot_general | solution.py:29
  178.6 9.7 %fusion.41 = f32[2304,1,1,256]{3,0,2,1:T(8,128)S(1)} fusion(f32[256,2304]{0,1:T(8,128)S(1)} %fusion.6, f32[576,256]{1,0:T(8,128)S(1)} %fusion.98, f32[2,1,576,2304]{3,2,1,0:T(8,128)S(1)} %bitcast.238), kind=kOutput, calls=%fused_computation.44 | convolution fusion | flops 4077453312 | bytes 10616832 | tf_op jit(solution)/shard_map/frk,frc->kfc/dot_general | solution.py:26
  188.3 9.9 %fusion.38 = f32[2304,1,1,256]{3,0,2,1:T(8,128)S(1)} fusion(f32[256,2304]{0,1:T(8,128)S(1)} %fusion.4, f32[576,256]{1,0:T(8,128)S(1)} %fusion.101, f32[2,1,576,2304]{3,2,1,0:T(8,128)S(1)} %bitcast.238), kind=kOutput, calls=%fused_computation.43 | convolution fusion | flops 4077453312 | bytes 10616832 | tf_op jit(solution)/shard_map/frk,frc->kfc/dot_general | solution.py:29
  203.1 170.4 %all-reduce.3.cloned.1.call-done = f32[2304,2,1,256]{3,0,2,1:T(8,128)} async-done(((f32[2304,2,1,256]{3,0,2,1:T(8,128)}), f32[2304,2,1,256]{3,0,2,1:T(8,128)}) %all-reduce.3.cloned.1.call-update) | async-done | bytes 4718608 | tf_op jit(solution)/shard_map/psum | solution.py:91
  375.9 7.8 fusion
  383.7 7.0 fusion.2
  396.4 6.3 fusion.109
  402.7 39.0 %all-reduce = (f32[]{:T(128)}, f32[]{:T(128)}) all-reduce(f32[]{:T(128)} %get-tuple-element.8, f32[]{:T(128)} %fusion.109), channel_id=1, replica_groups=mesh['freq'=8,'rcv'=4] {'freq','rcv'}, use_global_device_ids=true, to_apply=%region_2.3 | all-reduce | flops 2 | bytes 16 | tf_op jit(solution)/shard_map/psum | solution.py:102
  448.0 31.0 %scatter_fusion = f32[2,576,2304]{1,0,2:T(2,128)} fusion(f32[2,576,2304]{1,0,2:T(2,128)} %bitcast.242, s32[256]{0:T(256)S(1)} %compare_select_fusion, f32[256,2,576]{2,1,0:T(2,128)S(1)} %copy.36), kind=kCustom, calls=%fused_computation.1 | custom fusion | flops 294912 | bytes 3539968 | tf_op jit(solution)/shard_map/scatter-add | solution.py:104
  479.0 21.2 %copy.37 = f32[2,1,576,2304]{3,0,1,2:T(2,128)} copy(f32[2,1,576,2304]{2,0,3,1:T(2,128)} %bitcast.243) | data formatting | bytes 21233664 | tf_op jit(solution)/shard_map/scatter-add | solution.py:104
  500.2 6.4 all-to-all-start
  507.3 113.8 %all-to-all-done = f32[2,1,576,2304]{3,0,1,2:T(2,128)} async-done(((f32[2,1,576,2304]{3,0,1,2:T(2,128)}), f32[2,1,576,2304]{3,0,1,2:T(2,128)}, u32[]{:S(2)}, u32[]{:S(2)}) %all-to-all-start) | async-done | bytes 10616864 | tf_op jit(solution)/shard_map/all_to_all | solution.py:106
  621.1 12.6 %fusion.174 = (f32[1,1,576,2304]{3,0,1,2:T(1,128)S(1)}, f32[1,1,576,2304]{3,0,1,2:T(1,128)S(1)}) fusion(f32[2,1,576,2304]{3,0,1,2:T(2,128)} %all-to-all-done), kind=kLoop, calls=%fused_computation.145 | loop fusion | bytes 21233664 | tf_op jit(solution)/shard_map/slice | solution.py:44
  634.1 7.0 fusion.30
  641.1 7.0 fusion.28
  648.5 7.1 convolution_subtract_fusion
  655.6 7.4 convolution_add_fusion
  663.0 7.6 fusion.121
  670.7 8.0 fusion.119
  678.7 8.8 %multiply_bitcast_fusion.1 = f32[1,8,72,2304]{3,1,2,0:T(8,128)} fusion(f32[8,72,2304]{2,0,1:T(8,128)S(1)} %fusion.121, f32[8,72,2304]{2,0,1:T(8,128)S(1)} %convolution_add_fusion, f32[8,72,2304]{2,0,1:T(8,128)S(1)} %convolution_subtract_fusion, f32[8,2304]{1,0:T(8,128)S(1)} %convert_element_type.21, f32[]{:T(128)} %bitcast.234), kind=kOutput, calls=%fused_computation.28 | convolution fusion | flops 142001024 | bytes 21307396 | tf_op jit(solution)/shard_map/tf,f...->t.../dot_general | solution.py:57
  687.5 9.0 %multiply_bitcast_fusion = f32[1,8,72,2304]{3,1,2,0:T(8,128)} fusion(f32[8,72,2304]{2,0,1:T(8,128)S(1)} %fusion.119, f32[8,72,2304]{2,0,1:T(8,128)S(1)} %convolution_subtract_fusion, f32[8,72,2304]{2,0,1:T(8,128)S(1)} %convolution_add_fusion, f32[8,2304]{1,0:T(8,128)S(1)} %convert_element_type.21, f32[]{:T(128)} %bitcast.235), kind=kOutput, calls=%fused_computation.27 | convolution fusion | flops 142001024 | bytes 21307396 | tf_op jit(solution)/shard_map/tf,f...->t.../dot_general | solution.py:61
  701.2 7.4 copy.44
  708.6 8.6 %all-to-all-start.1 = ((f32[2,8,72,2304]{3,2,0,1:T(8,128)}), f32[2,8,72,2304]{3,2,0,1:T(8,128)}, u32[]{:S(2)}, u32[]{:S(2)}) async-start(f32[2,8,72,2304]{3,2,0,1:T(8,128)} %copy.44), calls=%async_computation.1 | async-start | bytes 21233664 | tf_op jit(solution)/shard_map/all_to_all | solution.py:108
  718.4 113.3 %all-to-all-done.1 = f32[2,8,72,2304]{3,2,0,1:T(8,128)} async-done(((f32[2,8,72,2304]{3,2,0,1:T(8,128)}), f32[2,8,72,2304]{3,2,0,1:T(8,128)}, u32[]{:S(2)}, u32[]{:S(2)}) %all-to-all-start.1) | async-done | bytes 10616864 | tf_op jit(solution)/shard_map/all_to_all | solution.py:108
  831.7 9.0 %copy.45 = f32[2,8,72,2304]{3,2,1,0:T(8,128)} copy(f32[2,8,72,2304]{3,2,0,1:T(8,128)} %all-to-all-done.1) | data formatting | bytes 21233664 | tf_op jit(solution)/shard_map/all_to_all | solution.py:108
  (54 shorter events, 35.0 us)
Async XLA Ops:
  7.2 121.1 %all-gather.2.cloned.1.call-start = ((), (), s32[]{:S(2)}) async-start(), calls=%async_computation.2 | async-start | bytes 5898240 | tf_op jit(solution)/shard_map/all_gather | solution.py:72
  27.8 9.3 %copy-start.5 = (f32[2,1]{0,1:T(1,128)S(1)}, f32[2,1]{0,1:T(1,128)}, u32[]{:S(2)}) copy-start(f32[2,1]{0,1:T(1,128)} %param.10) | copy-start | bytes 28
  36.7 99.1 %copy-start.2 = (f32[2,1,576,256]{3,2,1,0:T(8,128)S(1)}, f32[2,1,576,256]{3,2,1,0:T(8,128)}, u32[]{:S(2)}) copy-start(f32[2,1,576,256]{3,2,1,0:T(8,128)} %bitcast_select_fusion) | copy-start | bytes 3538948
  36.8 336.8 %all-reduce.3.cloned.1.call-start = ((), (), s32[]{:S(2)}) async-start(), calls=%async_computation.3 | async-start | bytes 9437184 | tf_op jit(solution)/shard_map/psum | solution.py:91
  128.3 29.2 %slice-start = ((s8[10616832]{0:T(1024)(128)(4,1)}), s8[4194304]{0:T(1024)(128)(4,1)S(1)}, s32[]{:S(2)}) async-start(s8[10616832]{0:T(1024)(128)(4,1)} %bitcast.237), calls=%async_computation.4 | async-start | bytes 8388608
  128.3 29.2 %slice-start.6 = ((s8[4718592]{0:T(1024)(128)(4,1)}), s8[4194304]{0:T(1024)(128)(4,1)S(1)}, s32[]{:S(2)}) async-start(s8[4718592]{0:T(1024)(128)(4,1)} %bitcast.248), calls=%async_computation.10 | async-start | bytes 8388608
  135.8 21.7 %slice-start.1 = ((s8[10616832]{0:T(1024)(128)(4,1)}), s8[4194304]{0:T(1024)(128)(4,1)S(1)}, s32[]{:S(2)}) async-start(s8[10616832]{0:T(1024)(128)(4,1)} %bitcast.237), calls=%async_computation.5 | async-start | bytes 8388608
  135.8 21.7 %slice-start.2 = ((s8[10616832]{0:T(1024)(128)(4,1)}), s8[2228224]{0:T(1024)(128)(4,1)S(1)}, s32[]{:S(2)}) async-start(s8[10616832]{0:T(1024)(128)(4,1)} %bitcast.237), calls=%async_computation.6 | async-start | bytes 4456448
  135.8 21.7 %slice-start.7 = ((s8[4718592]{0:T(1024)(128)(4,1)}), s8[524288]{0:T(1024)(128)(4,1)S(1)}, s32[]{:S(2)}) async-start(s8[4718592]{0:T(1024)(128)(4,1)} %bitcast.248), calls=%async_computation.11 | async-start | bytes 1048576
  157.5 4.4 copy-start.3
  203.1 187.6 %slice-start.3 = ((s8[10616832]{0:T(1024)(128)(4,1)}), s8[2228224]{0:T(1024)(128)(4,1)S(1)}, s32[]{:S(2)}) async-start(s8[10616832]{0:T(1024)(128)(4,1)} %bitcast.239), calls=%async_computation.7 | async-start | bytes 4456448
  373.5 10.2 %copy-start = (f32[2304,2,1,256]{3,0,2,1:T(8,128)S(1)}, f32[2304,2,1,256]{3,0,2,1:T(8,128)}, u32[]{:S(2)}) copy-start(f32[2304,2,1,256]{3,0,2,1:T(8,128)} %all-reduce.3.cloned.1.call-done) | copy-start | bytes 14155780
  375.9 20.5 %copy-start.1 = (f32[2,1,576,256]{3,2,1,0:T(8,128)}, f32[2,1,576,256]{3,2,1,0:T(8,128)S(1)}, u32[]{:S(2)}) copy-start(f32[2,1,576,256]{3,2,1,0:T(8,128)S(1)} %get-tuple-element.9) | copy-start | bytes 3538948
  375.9 14.8 %slice-start.4 = ((s8[10616832]{0:T(1024)(128)(4,1)}), s8[4194304]{0:T(1024)(128)(4,1)S(1)}, s32[]{:S(2)}) async-start(s8[10616832]{0:T(1024)(128)(4,1)} %bitcast.239), calls=%async_computation.8 | async-start | bytes 8388608
  383.7 7.0 slice-start.5
  500.2 6.4 copy-start.4
  500.2 120.8 %all-to-all-start = ((f32[2,1,576,2304]{3,0,1,2:T(2,128)}), f32[2,1,576,2304]{3,0,1,2:T(2,128)}, u32[]{:S(2)}, u32[]{:S(2)}) async-start(f32[2,1,576,2304]{3,0,1,2:T(2,128)} %copy.37), calls=%async_computation | async-start | bytes 21233664 | tf_op jit(solution)/shard_map/all_to_all | solution.py:106
  708.6 123.1 %all-to-all-start.1 = ((f32[2,8,72,2304]{3,2,0,1:T(8,128)}), f32[2,8,72,2304]{3,2,0,1:T(8,128)}, u32[]{:S(2)}, u32[]{:S(2)}) async-start(f32[2,8,72,2304]{3,2,0,1:T(8,128)} %copy.44), calls=%async_computation.1 | async-start | bytes 21233664 | tf_op jit(solution)/shard_map/all_to_all | solution.py:108
Sparse Core Ops, SparseCore 0:
  36.9 91.3 all-gather.1
  203.2 170.2 all-reduce.2
where the time goes:
time: 856 us; the launch traced here: 848 us
  waiting for transfers between devices  488 us (57%)
  matrix products  157 us (18%)
  local copies, waits for them, and re-layouts  81.3 us (9%)
  other arithmetic  50.3 us (6%)
  blocking collectives  39 us (5%)
  between operations  16.6 us (2%)
  starting transfers between devices  15.4 us (2%)
    psum x1, waiting for transfers between devices, on_device(): summed_all = lax.psum(summed_terms, 'rcv')  170 us
    all_to_all x1, waiting for transfers between devices, on_device(): lax.all_to_all(updated, 'freq', split_axis=2, concat_axis=1, tiled=True)  114 us
    all_to_all x1, waiting for transfers between devices, on_device(): lax.all_to_all(shrunk, 'freq', split_axis=1, concat_axis=2, tiled=True)  113 us
    all_gather x1, waiting for transfers between devices, on_device(): shard_piece = lax.all_gather(picked, 'rcv', axis=2, tiled=True)  90.5 us
    psum x1, blocking collectives, on_device(): totals = lax.psum((norm_dir, norm_img), ('freq', 'rcv'))  39 us
    scatter-add x1, other arithmetic, on_device(): updated = green_freq.at[:, :, :, sources].add(step_size * direction)  31 us
    scatter-add x1, local copies, waits for them, and re-layouts, on_device(): updated = green_freq.at[:, :, :, sources].add(step_size * direction)  21.2 us
    unnamed x31, local copies, waits for them, and re-layouts  20 us
  transfers between devices with their start and end apart: 4, of which 4 were waited for; matrix products, arithmetic and copies ran while one was open for 0% of the time, Pallas kernels for 0%

commit v1 on v0

v1 whole, which is shorter than its diff:
```python
import functools
import math

import jax
import jax.numpy as jnp
from jax import lax
from jax.experimental import pallas as pl
from jax.experimental.pallas import tpu as pltpu
from jax.sharding import PartitionSpec as P

HIGH = lax.Precision.HIGH
MESH = pl.DeviceIdType.MESH


def transform(points, sign):
    count = len(points)
    if count == 1:
        return points
    if count % 2:
        out = []
        for t in range(count):
            real, imag = points[0]
            for f in range(1, count):
                angle = sign * 2.0 * math.pi * (f * t % count) / count
                c, s = math.cos(angle), math.sin(angle)
                real = real + (c * points[f][0] - s * points[f][1])
                imag = imag + (s * points[f][0] + c * points[f][1])
            out.append((real, imag))
        return out
    even = transform(points[0::2], sign)
    odd = transform(points[1::2], sign)
    low, high = [], []
    for k in range(count // 2):
        er, ei = even[k]
        r, i = odd[k]
        angle = 8 * k / count
        if k == 0:
            tr, ti = r, i
        elif angle == 2:
            tr, ti = (-i, r) if sign > 0 else (i, -r)
        elif angle == 1:
            h = math.sqrt(0.5)
            tr, ti = (h * (r - i), h * (r + i)) if sign > 0 else (h * (r + i), h * (i - r))
        elif angle == 3:
            h = math.sqrt(0.5)
            tr, ti = (-h * (r + i), h * (r - i)) if sign > 0 else (h * (i - r), -h * (r + i))
        else:
            c = math.cos(2 * math.pi * k / count)
            s = sign * math.sin(2 * math.pi * k / count)
            tr, ti = c * r - s * i, s * r + c * i
        low.append((er + tr, ei + ti))
        high.append((er - tr, ei - ti))
    return low + high


def shrink_points(points, keep, level):
    count = len(points)
    timed = transform(points, 1)
    kept = []
    for t, (real, imag) in enumerate(timed):
        size = jnp.sqrt(real * real + imag * imag)
        factor = jnp.maximum(size - level, 0.0) / jnp.maximum(size, level) * keep[t : t + 1]
        factor = factor * (1.0 / count)
        kept.append((factor * real, factor * imag))
    return transform(kept, -1)


def shrink_body(scal_ref, keep_ref, *refs):
    *x_refs, o_ref = refs
    x_ref = x_refs[0]
    count = x_ref.shape[1]
    level = scal_ref[0]

    def lanes(j, carry):
        at = pl.ds(pl.multiple_of(j * 128, 128), 128)
        points = [(x_ref[0, f, :, at], x_ref[1, f, :, at]) for f in range(count)]
        if len(x_refs) == 2:
            d_ref = x_refs[1]
            step = scal_ref[1]
            points = [
                (r + step * d_ref[0, f, :, at], i + step * d_ref[1, f, :, at])
                for f, (r, i) in enumerate(points)
            ]
        out = shrink_points(points, keep_ref[:, at], level)
        for f in range(count):
            o_ref[0, f, :, at] = out[f][0]
            o_ref[1, f, :, at] = out[f][1]
        return carry

    lax.fori_loop(0, x_ref.shape[3] // 128, lanes, 0)


def shrink_call(scalars, keep, arrays):
    two, count, rows, width = arrays[0].shape
    tile = 8 if rows % 8 == 0 else rows
    if rows % 24 == 0 and width <= 512:
        tile = 24
    block = pl.BlockSpec((two, count, tile, width), lambda j: (0, 0, j, 0))
    size = arrays[0].size * 4
    return pl.pallas_call(
        shrink_body,
        grid=(rows // tile,),
        in_specs=[
            pl.BlockSpec(memory_space=pltpu.SMEM),
            pl.BlockSpec((count, width), lambda j: (0, 0)),
        ]
        + [block] * len(arrays),
        out_specs=block,
        out_shape=jax.ShapeDtypeStruct(arrays[0].shape, jnp.float32),
        cost_estimate=pl.CostEstimate(
            flops=40 * arrays[0].size, bytes_accessed=size * (1 + len(arrays)), transcendentals=0
        ),
    )(scalars, keep, *arrays)


def merge_body(mask_ref, hot_ref, cols_ref, back_ref, o_ref):
    hot = hot_ref[...]
    mask = mask_ref[...] > 0.5
    for part in range(2):
        x = cols_ref[:, part * hot.shape[0] : (part + 1) * hot.shape[0]]
        hi = x.astype(jnp.bfloat16)
        rest = x - hi.astype(jnp.float32)
        mid = rest.astype(jnp.bfloat16)
        low = (rest - mid.astype(jnp.float32)).astype(jnp.bfloat16)
        spread = (
            jnp.dot(hi, hot, preferred_element_type=jnp.float32)
            + jnp.dot(mid, hot, preferred_element_type=jnp.float32)
        ) + jnp.dot(low, hot, preferred_element_type=jnp.float32)
        o_ref[part, 0] = jnp.where(mask, spread, back_ref[part, 0])


def merge_call(mask, hot, cols, back):
    two, one, rows, width = back.shape
    picked = hot.shape[0]
    tile = rows // 4 if rows % 32 == 0 else rows
    return pl.pallas_call(
        merge_body,
        grid=(rows // tile,),
        in_specs=[
            pl.BlockSpec((1, width), lambda i: (0, 0)),
            pl.BlockSpec((picked, width), lambda i: (0, 0)),
            pl.BlockSpec((tile, two * picked), lambda i: (i, 0)),
            pl.BlockSpec((two, one, tile, width), lambda i: (0, 0, i, 0)),
        ],
        out_specs=pl.BlockSpec((two, one, tile, width), lambda i: (0, 0, i, 0)),
        out_shape=jax.ShapeDtypeStruct(back.shape, jnp.float32),
    )(mask, hot, cols, back)


def dots(lhs, rhs, contract):
    return lax.dot_general(lhs, rhs, (contract, ((), ())), precision=HIGH)


def apply_rows(data_real, data_imag, both, flipped):
    ahead = (((1,), (0,)))
    return dots(data_real, both, ahead) + dots(data_imag, flipped, ahead)


def ring_place(z, size):
    return jnp.where(z % 2 == 0, z // 2, size - 1 - z // 2)


def ring_owner(place, size):
    return jnp.where(2 * place < size, 2 * place, 2 * (size - 1 - place) + 1)


def ring_neighbours(size):
    z = lax.axis_index("rcv")
    place = ring_place(z, size)
    after = ring_owner((place + 1) % size, size)
    before = ring_owner((place + size - 1) % size, size)
    return z, place, after, before


def greet(freqs, after=None, before=None):
    me = lax.axis_index("freq")
    barrier = pltpu.get_barrier_semaphore()
    waits = freqs - 1
    for k in range(1, freqs):
        pl.semaphore_signal(
            barrier, inc=1, device_id={"freq": (me + k) % freqs}, device_id_type=MESH
        )
    if after is not None:
        for other in (after, before):
            pl.semaphore_signal(barrier, inc=1, device_id={"rcv": other}, device_id_type=MESH)
        waits += 2
    pl.semaphore_wait(barrier, waits)


def start_split(freqs, src, dst, sends, recvs, own):
    me = lax.axis_index("freq")
    rows = dst.shape[2]

    def part(j):
        return src.at[:, 0, pl.ds(pl.multiple_of(j * rows, 8), rows), :]

    copies = []
    for k in range(1, freqs):
        to = (me + k) % freqs
        copies.append(
            pltpu.make_async_remote_copy(
                part(to), dst.at[:, me], sends.at[k], recvs.at[k],
                device_id={"freq": to}, device_id_type=MESH,
            )
        )
    copies.append(pltpu.make_async_copy(part(me), dst.at[:, me], own))
    for copy in copies:
        copy.start()
    return copies


def start_join(freqs, src, dst, sends, recvs, own):
    me = lax.axis_index("freq")
    rows = src.shape[2]
    land = dst.at[:, 0, pl.ds(pl.multiple_of(me * rows, 8), rows), :]
    copies = []
    for k in range(1, freqs):
        to = (me + k) % freqs
        copies.append(
            pltpu.make_async_remote_copy(
                src.at[:, to], land, sends.at[k], recvs.at[k],
                device_id={"freq": to}, device_id_type=MESH,
            )
        )
    copies.append(pltpu.make_async_copy(src.at[:, me], land, own))
    for copy in copies:
        copy.start()
    return copies


def start_rows(freqs, src, dst, sends, recvs, own):
    me = lax.axis_index("freq")
    rows = dst.shape[1]

    def part(j):
        return src.at[pl.ds(pl.multiple_of(j * rows, 8), rows), :]

    copies = []
    for k in range(1, freqs):
        to = (me + k) % freqs
        copies.append(
            pltpu.make_async_remote_copy(
                part(to), dst.at[me], sends.at[k], recvs.at[k],
                device_id={"freq": to}, device_id_type=MESH,
            )
        )
    copies.append(pltpu.make_async_copy(part(me), dst.at[me], own))
    for copy in copies:
        copy.start()
    return copies


def ring_gather(size, place, after, blocks, sends, recvs):
    for step in range(size - 1):
        at = ring_owner((place + size - step) % size, size)
        copy = pltpu.make_async_remote_copy(
            blocks.at[at], blocks.at[at], sends.at[step], recvs.at[step],
            device_id={"rcv": after}, device_id_type=MESH,
        )
        copy.start()
        copy.wait()


def first_body(freqs, size, green, picked, gathered, whole, sends, recvs, own, rsend, rrecv):
    z, place, after, before = ring_neighbours(size)
    whole[z] = picked[...]
    greet(freqs, after, before)
    copies = start_split(freqs, green, gathered, sends, recvs, own)
    ring_gather(size, place, after, whole, rsend, rrecv)
    for copy in copies:
        copy.wait()


def second_body(
    freqs, size, shrunk, adjoint, local, picked, back, dir_all, dir_timed, pick_timed,
    held, total, sends, recvs, own, rsend, rrecv, gsend, grecv, dsend, drecv, down, psend, precv, pown,
):
    me = lax.axis_index("freq")
    z, place, after, before = ring_neighbours(size)
    greet(freqs, after, before)
    copies = start_join(freqs, shrunk, back, sends, recvs, own)
    copies += start_rows(freqs, picked, pick_timed, psend, precv, pown)
    for step in range(size - 1):
        at = ring_owner((place + 2 * size - 1 - step) % size, size)
        if step:
            total[step - 1] = held[step - 1] + adjoint[at]
        copy = pltpu.make_async_remote_copy(
            adjoint.at[at] if step == 0 else total.at[step - 1],
            held.at[step], rsend.at[step], rrecv.at[step],
            device_id={"rcv": after}, device_id_type=MESH,
        )
        copy.start()
        copy.wait()
    dir_all[z] = local[...] - (held[size - 2] + adjoint[z])
    copies += start_rows(freqs, dir_all.at[z], dir_timed, dsend, drecv, down)
    ring_gather(size, place, after, dir_all, gsend, grecv)
    for copy in copies:
        copy.wait()


def third_body(
    freqs, size, level_ref, norms, keep, picks, dirs, out,
    freq_box, rcv_box, cols, fsend, frecv, zsend, zrecv, sends, recvs, own,
):
    me = lax.axis_index("freq")
    z = lax.axis_index("rcv")
    barrier = pltpu.get_barrier_semaphore()
    for k in range(1, freqs):
        pl.semaphore_signal(
            barrier, inc=1, device_id={"freq": (me + k) % freqs}, device_id_type=MESH
        )
    for k in range(1, size):
        pl.semaphore_signal(barrier, inc=1, device_id={"rcv": (z + k) % size}, device_id_type=MESH)
    pl.semaphore_wait(barrier, freqs + size - 2)

    copies = []
    for k in range(1, freqs):
        copies.append(
            pltpu.make_async_remote_copy(
                norms, freq_box.at[k], fsend.at[k], frecv.at[k],
                device_id={"freq": (me + k) % freqs}, device_id_type=MESH,
            )
        )
    for copy in copies:
        copy.start()
    for copy in copies:
        copy.wait()
    parts = norms[...]
    for k in range(1, freqs):
        parts = parts + freq_box[k]
    rcv_box[0] = parts
    copies = []
    for k in range(1, size):
        copies.append(
            pltpu.make_async_remote_copy(
                rcv_box.at[0], rcv_box.at[k], zsend.at[k], zrecv.at[k],
                device_id={"rcv": (z + k) % size}, device_id_type=MESH,
            )
        )
    for copy in copies:
        copy.start()
    for copy in copies:
        copy.wait()
    total = rcv_box[0]
    for k in range(1, size):
        total = total + rcv_box[k]
    step = total[0] / total[1]
    level = level_ref[0]
    count = picks.shape[2] // 2

    def tile(i, carry):
        rows = pl.ds(pl.multiple_of(i * 8, 8), 8)
        for lane in range(0, count, 128):
            re = slice(lane, lane + 128)
            im = slice(count + lane, count + lane + 128)
            points = [
                (
                    picks[f, rows, re] + step * dirs[f, rows, re],
                    picks[f, rows, im] + step * dirs[f, rows, im],
                )
                for f in range(freqs)
            ]
            done = shrink_points(points, keep[:, re], level)
            for f in range(freqs):
                cols[f, rows, re] = done[f][0]
                cols[f, rows, im] = done[f][1]
        return carry

    lax.fori_loop(0, picks.shape[1] // 8, tile, 0)
    rows = cols.shape[1]
    land = out.at[pl.ds(pl.multiple_of(me * rows, 8), rows), :]
    copies = []
    for k in range(1, freqs):
        to = (me + k) % freqs
        copies.append(
            pltpu.make_async_remote_copy(
                cols.at[to], land, sends.at[k], recvs.at[k],
                device_id={"freq": to}, device_id_type=MESH,
            )
        )
    copies.append(pltpu.make_async_copy(cols.at[me], land, own))
    for copy in copies:
        copy.start()
    for copy in copies:
        copy.wait()


ANY = pl.BlockSpec(memory_space=pltpu.HBM)
VMEM = pl.BlockSpec(memory_space=pltpu.VMEM)
DMA = pltpu.SemaphoreType.DMA


def first_call(freqs, size, green, picked):
    two, _, rows, width = green.shape
    return pl.pallas_call(
        functools.partial(first_body, freqs, size),
        out_shape=(
            jax.ShapeDtypeStruct((two, freqs, rows // freqs, width), jnp.float32),
            jax.ShapeDtypeStruct((size,) + picked.shape, jnp.float32),
        ),
        in_specs=[ANY, VMEM],
        out_specs=(ANY, VMEM),
        scratch_shapes=[DMA((freqs,)), DMA((freqs,)), DMA(()), DMA((size,)), DMA((size,))],
        compiler_params=pltpu.CompilerParams(
            collective_id=0, has_side_effects=True, vmem_limit_bytes=40 << 20
        ),
    )(green, picked)


def second_call(freqs, size, shrunk, adjoint, local, picked):
    two, _, part, width = shrunk.shape
    rows, both = local.shape
    pair = [DMA((freqs,)), DMA((freqs,)), DMA(())]
    ring = [DMA((size,)), DMA((size,))]
    return pl.pallas_call(
        functools.partial(second_body, freqs, size),
        out_shape=(
            jax.ShapeDtypeStruct((two, 1, rows, width), jnp.float32),
            jax.ShapeDtypeStruct((size, rows, both), jnp.float32),
            jax.ShapeDtypeStruct((freqs, part, both), jnp.float32),
            jax.ShapeDtypeStruct((freqs, part, both), jnp.float32),
        ),
        in_specs=[ANY, VMEM, VMEM, VMEM],
        out_specs=(ANY, VMEM, VMEM, VMEM),
        scratch_shapes=[
            pltpu.VMEM((size - 1, rows, both), jnp.float32),
            pltpu.VMEM((size - 2, rows, both), jnp.float32),
        ]
        + pair + ring + ring + pair + pair,
        compiler_params=pltpu.CompilerParams(
            collective_id=1, has_side_effects=True, vmem_limit_bytes=48 << 20
        ),
    )(shrunk, adjoint, local, picked)


def third_call(freqs, size, level, norms, keep, picks, dirs):
    _, part, both = picks.shape
    return pl.pallas_call(
        functools.partial(third_body, freqs, size),
        out_shape=jax.ShapeDtypeStruct((part * freqs, both), jnp.float32),
        in_specs=[pl.BlockSpec(memory_space=pltpu.SMEM), VMEM, VMEM, VMEM, VMEM],
        out_specs=VMEM,
        scratch_shapes=[
            pltpu.VMEM((freqs, 2, 8, 128), jnp.float32),
            pltpu.VMEM((size, 2, 8, 128), jnp.float32),
            pltpu.VMEM((freqs, part, both), jnp.float32),
            DMA((freqs,)), DMA((freqs,)), DMA((size,)), DMA((size,)),
            DMA((freqs,)), DMA((freqs,)), DMA(()),
        ],
        compiler_params=pltpu.CompilerParams(
            collective_id=2, has_side_effects=True, vmem_limit_bytes=32 << 20
        ),
    )(level, norms, keep, picks, dirs)


def pick_body(hot_ref, x_ref, o_ref):
    picks = hot_ref.shape[1]
    hot = hot_ref[...]
    for part in range(2):
        x = x_ref[part, 0]
        hi = x.astype(jnp.bfloat16)
        rest = x - hi.astype(jnp.float32)
        mid = rest.astype(jnp.bfloat16)
        low = (rest - mid.astype(jnp.float32)).astype(jnp.bfloat16)
        o_ref[:, part * picks : (part + 1) * picks] = (
            jnp.dot(hi, hot, preferred_element_type=jnp.float32)
            + jnp.dot(mid, hot, preferred_element_type=jnp.float32)
        ) + jnp.dot(low, hot, preferred_element_type=jnp.float32)


def pick_call(hot, green):
    two, one, rows, width = green.shape
    picks = hot.shape[1]
    tile = rows // 4 if rows % 32 == 0 else rows
    return pl.pallas_call(
        pick_body,
        grid=(rows // tile,),
        in_specs=[
            pl.BlockSpec((width, picks), lambda i: (0, 0)),
            pl.BlockSpec((two, one, tile, width), lambda i: (0, 0, i, 0)),
        ],
        out_specs=pl.BlockSpec((tile, 2 * picks), lambda i: (i, 0)),
        out_shape=jax.ShapeDtypeStruct((rows, 2 * picks), jnp.float32),
    )(hot, green)


def on_device(green_freq, data_matrix, shot_panels, wavelet, sources, support, threshold):
    width = green_freq.shape[3]
    rows_here = green_freq.shape[2]
    picks = sources.shape[0]
    keep_all = support.astype(jnp.float32)
    freqs = lax.axis_size("freq")
    size = lax.axis_size("rcv")
    fast = rows_here % (8 * freqs) == 0 and size % 2 == 0 and size > 2
    places = jnp.arange(width, dtype=jnp.int32)
    pickcat = pick_call((places[:, None] == sources[None, :]).astype(jnp.bfloat16), green_freq)
    picked = (pickcat[:, :picks], pickcat[:, picks:])
    if fast:
        gathered, both = first_call(freqs, size, green_freq, pickcat)
        both = both.reshape(size * rows_here, 2 * picks)
    else:
        gathered = lax.all_to_all(green_freq, "freq", split_axis=2, concat_axis=1, tiled=True)
        both = lax.all_gather(pickcat, "rcv", axis=0, tiled=True)
    wr = wavelet[0, 0]
    wi = wavelet[1, 0]
    dr = data_matrix[0, 0]
    di = data_matrix[1, 0]
    flipped = jnp.concatenate([-both[:, picks:], both[:, :picks]], axis=1)
    multiple = apply_rows(dr, di, both, flipped)
    resid_real = shot_panels[0, 0] - (wr * picked[0] - wi * picked[1] - multiple[:, :picks])
    resid_imag = shot_panels[1, 0] - (wr * picked[1] + wi * picked[0] - multiple[:, picks:])
    residual = jnp.stack([resid_real, resid_imag])[:, None]
    down = ((0,), (0,))
    rboth = jnp.concatenate([resid_real, resid_imag], axis=1)
    rflip = jnp.concatenate([resid_imag, -resid_real], axis=1)
    adjoint = dots(dr, rboth, down) + dots(di, rflip, down)
    shrunk = shrink_call(threshold, keep_all, (gathered,))
    local = jnp.concatenate(
        [wr * resid_real + wi * resid_imag, wr * resid_imag - wi * resid_real], axis=1
    )
    if fast:
        back, dir_all, dir_timed, pick_timed = second_call(
            freqs, size, shrunk, adjoint.reshape(size, rows_here, 2 * picks), local, pickcat
        )
        direction = lax.dynamic_index_in_dim(dir_all, lax.axis_index("rcv"), 0, keepdims=False)
        dir_all = dir_all.reshape(size * rows_here, 2 * picks)
    else:
        reduced = lax.psum_scatter(adjoint, "rcv", scatter_dimension=0, tiled=True)
        direction = local - reduced
        dir_all = lax.all_gather(direction, "rcv", axis=0, tiled=True)
        back = lax.all_to_all(shrunk, "freq", split_axis=1, concat_axis=2, tiled=True)
        dir_timed = lax.all_to_all(
            jnp.stack([direction[:, :picks], direction[:, picks:]])[:, None],
            "freq", split_axis=2, concat_axis=1, tiled=True,
        )
    dir_real = direction[:, :picks]
    dir_imag = direction[:, picks:]
    pushed = apply_rows(
        dr, di, dir_all, jnp.concatenate([-dir_all[:, picks:], dir_all[:, :picks]], axis=1)
    )
    image_real = wr * dir_real - wi * dir_imag - pushed[:, :picks]
    image_imag = wr * dir_imag + wi * dir_real - pushed[:, picks:]
    norm_dir = jnp.sum(direction * direction)
    norm_img = jnp.sum(image_real * image_real + image_imag * image_imag)
    keep_cols = jnp.take(keep_all, sources, axis=1)
    norms = jnp.stack([norm_dir, norm_img])
    if fast:
        cols_back = third_call(
            freqs, size, threshold, jnp.broadcast_to(norms[:, None, None], (2, 8, 128)),
            keep_cols, pick_timed, dir_timed,
        )
    else:
        totals = lax.psum(norms, ("freq", "rcv"))
        scalars = jnp.concatenate([threshold, (totals[0] / totals[1])[None]])
        pick_timed = jnp.take(gathered, sources, axis=3)
        cols = shrink_call(scalars, keep_cols, (pick_timed, dir_timed))
        cols_back = lax.all_to_all(cols, "freq", split_axis=1, concat_axis=2, tiled=True)
        cols_back = jnp.concatenate([cols_back[0, 0], cols_back[1, 0]], axis=1)
    hot = sources[:, None] == places[None, :]
    mask = jnp.any(hot, axis=0, keepdims=True).astype(jnp.float32)
    green_next = merge_call(mask, hot.astype(jnp.bfloat16), cols_back, back)
    return (green_next, residual)


def solution(mesh):
    in_specs = (
        P(None, "freq", "rcv", None),
        P(None, "freq", "rcv", None),
        P(None, "freq", "rcv", None),
        P(None, "freq"),
        P(),
        P(),
        P(),
    )
    out_specs = (P(None, "freq", "rcv", None), P(None, "freq", "rcv", None))
    return jax.shard_map(
        on_device, mesh=mesh, in_specs=in_specs, out_specs=out_specs, check_vma=False
    )
```

time: 856 us -> 413 us (0.48)
  waiting for transfers between devices: 488 us -> 0 us
  Pallas kernels: 0 us -> 346 us
  matrix products: 157 us -> 32.6 us
  local copies, waits for them, and re-layouts: 81.3 us -> 14.7 us
  blocking collectives: 39 us -> 0 us
  other arithmetic: 50.3 us -> 17.6 us
  starting transfers between devices: 15.4 us -> 0 us
  between operations: 16.6 us -> 1.62 us
    pallas_call x0 -> x6, Pallas kernels: none -> 346 us  [the longest x1 165 us: second_call(): pl.pallas_call(functools.partial(second_body, freqs, size), out_shape=(ja...]
    all_to_all x2 -> x0, waiting for transfers between devices: 227 us -> none  [the longest x1 114 us: on_device(): lax.all_to_all(updated, 'freq', split_axis=2, concat_axis=1, tiled=True)]
    psum x1 -> x0, waiting for transfers between devices: 170 us -> none  [on_device(): summed_all = lax.psum(summed_terms, 'rcv')]
    dot_general x20 -> x6, matrix products: 157 us -> 32.6 us  [dots(): return lax.dot_general(lhs, rhs, (contract, ((), ())), precision=HIGH)]
    all_gather x1 -> x0, waiting for transfers between devices: 90.5 us -> none  [on_device(): shard_piece = lax.all_gather(picked, 'rcv', axis=2, tiled=True)]
    psum x1 -> x0, blocking collectives: 39 us -> none  [on_device(): totals = lax.psum((norm_dir, norm_img), ('freq', 'rcv'))]
    scatter-add x1 -> x0, other arithmetic: 31 us -> none  [on_device(): updated = green_freq.at[:, :, :, sources].add(step_size * direction)]
    scatter-add x1 -> x0, local copies, waits for them, and re-layouts: 21.2 us -> none  [on_device(): updated = green_freq.at[:, :, :, sources].add(step_size * direction)]
  transfers between devices with their start and end apart: 4 -> 0, of which waited for: 4 -> 0; matrix products, arithmetic and copies ran while one was open for 0% -> 0% of each run, Pallas kernels for 0% -> 0%
where the time goes in v1:
time: 413 us; the launch traced here: 412 us
  Pallas kernels  346 us (84%)
  matrix products  32.6 us (8%)
  other arithmetic  17.6 us (4%)
  local copies, waits for them, and re-layouts  14.7 us (4%)
    pallas_call x1, Pallas kernels, second_call(): pl.pallas_call(functools.partial(second_body, freqs, size), out_shape=(ja...  165 us
    pallas_call x1, Pallas kernels, first_call(): pl.pallas_call(functools.partial(first_body, freqs, size), out_shape=(jax...  120 us
    dot_general x6, matrix products, dots(): return lax.dot_general(lhs, rhs, (contract, ((), ())), precision=HIGH)  32.6 us
    pallas_call x1, Pallas kernels, third_call(): pl.pallas_call(functools.partial(third_body, freqs, size), out_shape=jax....  28.3 us
    pallas_call x1, Pallas kernels, shrink_call(): pl.pallas_call(shrink_body, grid=(rows // tile,), in_specs=[pl.BlockSpec(...  13.6 us
    pallas_call x1, Pallas kernels, merge_call(): pl.pallas_call(merge_body, grid=(rows // tile,), in_specs=[pl.BlockSpec((...  11.2 us
    pallas_call x1, Pallas kernels, pick_call(): pl.pallas_call(pick_body, grid=(rows // tile,), in_specs=[pl.BlockSpec((w...  8.46 us

profile of v1, /device:TPU:1, one launch (start us, length us, event | category | flops | bytes accessed | tf_op | source)
XLA Modules:
  0.0 412.4 jit_solution(8927467047754937468)
XLA Ops:
  0.6 2.3 fusion.32.hot_ref
  2.9 8.5 %shard_map.86.picked = f32[576,512]{1,0:T(8,128)} custom-call(bf16[2304,256]{1,0:T(8,128)(2,1)} %fusion.32.hot_ref, f32[2,1,576,2304]{3,2,1,0:T(8,128)} %green.1), custom_call_target="tpu_custom_call" | custom-call | tf_op jit(solution)/shard_map/pallas_call | solution.py:475
  11.4 1.3 copy-done
  12.6 119.8 %shard_map.87 = (f32[2,8,72,2304]{3,2,1,0:T(8,128)}, f32[4,576,512]{2,1,0:T(8,128)S(1)}) custom-call(f32[2,1,576,2304]{3,2,1,0:T(8,128)} %green.1, f32[576,512]{1,0:T(8,128)S(1)} %copy-done), custom_call_target="tpu_custom_call" | custom-call | tf_op jit(solution)/shard_map/pallas_call | solution.py:395
  132.4 0.4 slice_negate_fusion.1
  132.8 1.2 slice-done.2
  134.1 4.4 %fusion.4 = f32[512,576]{0,1:T(8,128)S(1)} fusion(f32[2304,256]{1,0:T(8,128)S(1)} %get-tuple-element.24, f32[2304,256]{1,0:T(8,128)S(1)} %get-tuple-element.23, f32[2,1,576,2304]{3,2,1,0:T(8,128)S(1)} %bitcast.61), kind=kOutput, calls=%fused_computation.5 | convolution fusion | flops 4078043136 | bytes 11206656 | tf_op jit(solution)/shard_map/dot_general | solution.py:151
  138.5 4.3 %fusion.36 = f32[576,512]{1,0:T(8,128)S(1)} fusion(f32[512,576]{0,1:T(8,128)S(1)} %fusion.4, f32[2304,512]{1,0:T(8,128)S(1)} %bitcast.59, f32[2,1,576,2304]{3,2,1,0:T(8,128)S(1)} %bitcast.61), kind=kOutput, calls=%fused_computation.35 | convolution fusion | flops 4077158400 | bytes 12386304 | tf_op jit(solution)/shard_map/dot_general | solution.py:151
  142.8 0.6 fusion.63
  143.4 1.5 multiply_add_fusion
  144.9 1.2 multiply_subtract_fusion
  146.3 7.0 %fusion.2 = f32[512,2304]{1,0:T(8,128)S(1)} fusion(f32[2,1,576,2304]{3,2,1,0:T(8,128)S(1)} %bitcast.61, f32[576,256]{1,0:T(8,128)S(1)} %get-tuple-element.26, f32[576,256]{1,0:T(8,128)S(1)} %get-tuple-element.19), kind=kOutput, calls=%fused_computation.3 | convolution fusion | flops 4077158400 | bytes 11206656 | tf_op jit(solution)/shard_map/dot_general | solution.py:151
  153.3 8.1 %fusion.15 = f32[2304,512]{0,1:T(8,128)} fusion(f32[512,2304]{1,0:T(8,128)S(1)} %fusion.2, f32[2,1,576,2304]{3,2,1,0:T(8,128)S(1)} %bitcast.61, f32[576,256]{1,0:T(8,128)S(1)} %get-tuple-element.19, f32[576,256]{1,0:T(8,128)S(1)} %get-tuple-element.20), kind=kOutput, calls=%fused_computation.14 | convolution fusion | flops 4078338048 | bytes 15925248 | tf_op jit(solution)/shard_map/dot_general | solution.py:151
  161.4 6.1 %copy.9 = f32[2304,512]{1,0:T(8,128)} copy(f32[2304,512]{0,1:T(8,128)} %fusion.15) | data formatting | bytes 9437184 | tf_op jit(solution)/shard_map/add | solution.py:516
  167.5 0.6 convert_element_type.17.keep_ref
  168.8 13.6 %shard_map.88.shrunk = f32[2,8,72,2304]{3,2,1,0:T(8,128)} custom-call(f32[1]{0:T(128)S(6)} %copy.13.scal_ref.level_ref, f32[8,2304]{1,0:T(8,128)} %convert_element_type.17.keep_ref, f32[2,8,72,2304]{3,2,1,0:T(8,128)} %get-tuple-element.8.refs_0_), custom_call_target="tpu_custom_call" | custom-call | flops 106168320 | bytes 21233664 | tf_op jit(solution)/shard_map/pallas_call | solution.py:100
  182.4 164.6 %shard_map.89 = (f32[2,1,576,2304]{3,2,1,0:T(8,128)}, f32[4,576,512]{2,1,0:T(8,128)}, f32[8,72,512]{2,1,0:T(8,128)S(1)}, f32[8,72,512]{2,1,0:T(8,128)S(1)}) custom-call(f32[2,8,72,2304]{3,2,1,0:T(8,128)} %shard_map.88.shrunk, f32[4,576,512]{2,1,0:T(8,128)} %bitcast.68, f32[576,512]{1,0:T(8,128)S(1)} %pad_maximum_fusion.local, f32[576,512]{1,0:T(8,128)S(1)} %copy-done.1), custom_call_target="tpu_custom_call" | custom-call | tf_op jit(solution)/shard_map/pallas_call | solution.py:415
  347.0 3.2 slice_negate_fusion
  350.5 4.4 %fusion = f32[512,576]{0,1:T(8,128)S(1)} fusion(f32[2304,256]{1,0:T(8,128)S(1)} %get-tuple-element.22, f32[2304,256]{1,0:T(8,128)S(1)} %get-tuple-element.21, f32[2,1,576,2304]{3,2,1,0:T(8,128)S(1)} %bitcast.63), kind=kOutput, calls=%fused_computation.1 | convolution fusion | flops 4078043136 | bytes 11206656 | tf_op jit(solution)/shard_map/dot_general | solution.py:151
  354.9 4.4 %fusion.42 = f32[576,512]{1,0:T(8,128)S(1)} fusion(f32[512,576]{0,1:T(8,128)S(1)} %fusion, f32[2304,512]{1,0:T(8,128)S(1)} %bitcast.67, f32[2,1,576,2304]{3,2,1,0:T(8,128)S(1)} %bitcast.63), kind=kOutput, calls=%fused_computation.37 | convolution fusion | flops 4077158400 | bytes 12386304 | tf_op jit(solution)/shard_map/dot_general | solution.py:151
  359.3 2.2 multiply_reduce_fusion
  361.5 2.0 fusion.53
  363.5 1.3 pad_maximum_fusion.1
  364.8 1.2 copy.10
  366.1 1.3 gather_fusion
  367.5 1.0 copy.11
  368.5 28.3 %shard_map.90.cols_ref = f32[576,512]{1,0:T(8,128)S(1)} custom-call(f32[1]{0:T(128)S(6)} %copy.13.scal_ref.level_ref, f32[2,8,128]{2,1,0:T(8,128)S(1)} %broadcast_in_dim.26.norms, f32[8,256]{1,0:T(8,128)S(1)} %select_bitcast_fusion.keep, f32[8,72,512]{2,1,0:T(8,128)S(1)} %copy-done.4, f32[8,72,512]{2,1,0:T(8,128)S(1)} %get-tuple-element.12.dirs), custom_call_target="tpu_custom_call" | custom-call | tf_op jit(solution)/shard_map/pallas_call | solution.py:438
  396.8 1.0 copy-done.2
  397.8 1.6 fusion.30
  399.4 0.6 reshape.34.mask_ref
  400.1 11.2 %shard_map.91 = f32[2,1,576,2304]{3,2,1,0:T(8,128)} custom-call(f32[1,2304]{1,0:T(1,128)} %reshape.34.mask_ref, bf16[256,2304]{1,0:T(8,128)(2,1)} %get-tuple-element.27.hot_ref, f32[576,512]{1,0:T(8,128)} %copy-done.2, f32[2,1,576,2304]{3,2,1,0:T(8,128)} %get-tuple-element.13.back_ref), custom_call_target="tpu_custom_call" | custom-call | tf_op jit(solution)/shard_map/pallas_call | solution.py:136
  411.3 1.1 maximum_bitcast_fusion
  (49 shorter events, 0.6 us)
Async XLA Ops:
  11.3 1.3 copy-start
  12.6 120.2 %slice-start = ((s8[10616832]{0:T(1024)(128)(4,1)}), s8[4194304]{0:T(1024)(128)(4,1)S(1)}, s32[]{:S(2)}) async-start(s8[10616832]{0:T(1024)(128)(4,1)} %bitcast.60), calls=%async_computation | async-start | bytes 8388608
  12.6 120.2 %slice-start.1 = ((s8[10616832]{0:T(1024)(128)(4,1)}), s8[4194304]{0:T(1024)(128)(4,1)S(1)}, s32[]{:S(2)}) async-start(s8[10616832]{0:T(1024)(128)(4,1)} %bitcast.60), calls=%async_computation.1 | async-start | bytes 8388608
  132.4 1.6 slice-start.2
  138.4 4.4 %copy-start.12 = (f32[2,1]{0,1:T(1,128)S(1)}, f32[2,1]{0,1:T(1,128)}, u32[]{:S(2)}) copy-start(f32[2,1]{0,1:T(1,128)} %param.10) | copy-start | bytes 28
  138.5 4.9 %copy-start.9 = (f32[2,1,576,256]{3,2,1,0:T(8,128)S(1)}, f32[2,1,576,256]{3,2,1,0:T(8,128)}, u32[]{:S(2)}) copy-start(f32[2,1,576,256]{3,2,1,0:T(8,128)} %param.9) | copy-start | bytes 3538948
  144.9 8.5 %copy-start.5 = (f32[576,256]{1,0:T(8,128)}, f32[576,256]{1,0:T(8,128)S(1)}, u32[]{:S(2)}) copy-start(f32[576,256]{1,0:T(8,128)S(1)} %get-tuple-element.19) | copy-start | bytes 1769476
  144.9 8.5 %copy-start.7 = (f32[576,256]{1,0:T(8,128)}, f32[576,256]{1,0:T(8,128)S(1)}, u32[]{:S(2)}) copy-start(f32[576,256]{1,0:T(8,128)S(1)} %get-tuple-element.20) | copy-start | bytes 1769476
  161.4 6.1 %copy-start.10 = (s32[8,2304]{1,0:T(8,128)S(1)}, s32[8,2304]{1,0:T(8,128)}, u32[]{:S(2)}) copy-start(s32[8,2304]{1,0:T(8,128)} %param.12) | copy-start | bytes 221188
  168.8 13.6 %copy-start.1 = (f32[576,512]{1,0:T(8,128)S(1)}, f32[576,512]{1,0:T(8,128)}, u32[]{:S(2)}) copy-start(f32[576,512]{1,0:T(8,128)} %shard_map.86.picked) | copy-start | bytes 3538948
  182.4 167.8 %slice-start.3 = ((s8[10616832]{0:T(1024)(128)(4,1)}), s8[4194304]{0:T(1024)(128)(4,1)S(1)}, s32[]{:S(2)}) async-start(s8[10616832]{0:T(1024)(128)(4,1)} %bitcast.62), calls=%async_computation.3 | async-start | bytes 8388608
  182.4 167.8 %slice-start.4 = ((s8[10616832]{0:T(1024)(128)(4,1)}), s8[4194304]{0:T(1024)(128)(4,1)S(1)}, s32[]{:S(2)}) async-start(s8[10616832]{0:T(1024)(128)(4,1)} %bitcast.62), calls=%async_computation.4 | async-start | bytes 8388608
  347.0 3.2 copy-start.3
  347.0 3.5 slice-start.5
  347.0 7.8 %slice-start.6 = ((s8[4718592]{0:T(1024)(128)(4,1)}), s8[4194304]{0:T(1024)(128)(4,1)S(1)}, s32[]{:S(2)}) async-start(s8[4718592]{0:T(1024)(128)(4,1)} %bitcast.65), calls=%async_computation.6 | async-start | bytes 8388608
  350.5 4.4 %slice-start.7 = ((s8[4718592]{0:T(1024)(128)(4,1)}), s8[524288]{0:T(1024)(128)(4,1)S(1)}, s32[]{:S(2)}) async-start(s8[4718592]{0:T(1024)(128)(4,1)} %bitcast.65), calls=%async_computation.7 | async-start | bytes 1048576
  361.5 4.6 %copy-start.11 = (s32[256]{0:T(256)S(1)}, s32[256]{0:T(256)}, u32[]{:S(2)}) copy-start(s32[256]{0:T(256)} %param.11) | copy-start | bytes 3076
  361.5 7.0 %copy-start.4 = (f32[8,72,512]{2,1,0:T(8,128)S(1)}, f32[8,72,512]{2,1,0:T(8,128)}, u32[]{:S(2)}) copy-start(f32[8,72,512]{2,1,0:T(8,128)} %copy-done.3) | copy-start | bytes 3538948
  396.8 1.0 copy-start.2
  400.0 11.2 %copy-start.6 = (f32[576,256]{1,0:T(8,128)S(1)}, f32[576,256]{1,0:T(8,128)}, u32[]{:S(2)}) copy-start(f32[576,256]{1,0:T(8,128)} %copy-done.5) | copy-start | bytes 1769476
  400.0 11.2 %copy-start.8 = (f32[576,256]{1,0:T(8,128)S(1)}, f32[576,256]{1,0:T(8,128)}, u32[]{:S(2)}) copy-start(f32[576,256]{1,0:T(8,128)} %copy-done.7) | copy-start | bytes 1769476

commit v2 on v1

--- a/solution.py
+++ b/solution.py
@@ -251,49 +251,132 @@
 
 
 def ring_gather(size, place, after, blocks, sends, recvs):
+    rows = blocks.shape[0] // size
     for step in range(size - 1):
         at = ring_owner((place + size - step) % size, size)
+        part = blocks.at[pl.ds(pl.multiple_of(at * rows, 8), rows), :]
         copy = pltpu.make_async_remote_copy(
-            blocks.at[at], blocks.at[at], sends.at[step], recvs.at[step],
+            part, part, sends.at[step], recvs.at[step],
             device_id={"rcv": after}, device_id_type=MESH,
         )
         copy.start()
         copy.wait()
 
 
-def first_body(freqs, size, green, picked, gathered, whole, sends, recvs, own, rsend, rrecv):
+def halves(x):
+    hi = x.astype(jnp.bfloat16)
+    return hi, (x - hi.astype(jnp.float32)).astype(jnp.bfloat16)
+
+
+def product(lhs, rhs, contract):
+    lh, ll = lhs
+    rh, rl = rhs
+
+    def dot(x, y):
+        return lax.dot_general(x, y, (contract, ((), ())), preferred_element_type=jnp.float32)
+
+    return (dot(lh, rl) + dot(ll, rh)) + dot(lh, rh)
+
+
+CHUNK = 256
+
+
+def apply_data(data, x_ref, acc):
+    picks = x_ref.shape[1] // 2
+    acc[...] = jnp.zeros_like(acc)
+
+    def chunk(i, carry):
+        at = pl.ds(pl.multiple_of(i * CHUNK, CHUNK), CHUNK)
+        x = x_ref[at, :]
+        turned = jnp.concatenate([-x[:, picks:], x[:, :picks]], axis=1)
+        acc[...] += product(halves(data[0, :, at]), halves(x), ((1,), (0,)))
+        acc[...] += product(halves(data[1, :, at]), halves(turned), ((1,), (0,)))
+        return carry
+
+    lax.fori_loop(0, x_ref.shape[0] // CHUNK, chunk, 0)
+
+
+def apply_adjoint(data, x_ref, out):
+    picks = x_ref.shape[1] // 2
+    x = x_ref[...]
+    straight = halves(x)
+    turned = halves(jnp.concatenate([x[:, picks:], -x[:, :picks]], axis=1))
+
+    def chunk(i, carry):
+        at = pl.ds(pl.multiple_of(i * CHUNK, CHUNK), CHUNK)
+        out[at, :] = product(halves(data[0, :, at]), straight, ((0,), (0,))) + product(
+            halves(data[1, :, at]), turned, ((0,), (0,))
+        )
+        return carry
+
+    lax.fori_loop(0, out.shape[0] // CHUNK, chunk, 0)
+
+
+def first_body(
+    freqs, size, level, wave, green, picked, shots, keep, data_hbm,
+    gathered, shrunk, back, residual, norms, dir_timed, pick_timed,
+    whole, dir_all, adjoint, local, held, total, data, image,
+    fsend, frecv, fown, sends, recvs, own, arsend, arrecv, rsend, rrecv, gsend, grecv,
+    dsend, drecv, down, psend, precv, pown, load,
+):
     z, place, after, before = ring_neighbours(size)
-    whole[z] = picked[...]
+    rows, both = picked.shape
+    picks = both // 2
+
+    def part(at):
+        return pl.ds(pl.multiple_of(at * rows, 8), rows)
+
+    fetch = pltpu.make_async_copy(data_hbm.at[:, 0], data, load)
+    fetch.start()
+    whole[part(z), :] = picked[...]
     greet(freqs, after, before)
-    copies = start_split(freqs, green, gathered, sends, recvs, own)
-    ring_gather(size, place, after, whole, rsend, rrecv)
-    for copy in copies:
-        copy.wait()
-
-
-def second_body(
-    freqs, size, shrunk, adjoint, local, picked, back, dir_all, dir_timed, pick_timed,
-    held, total, sends, recvs, own, rsend, rrecv, gsend, grecv, dsend, drecv, down, psend, precv, pown,
-):
-    me = lax.axis_index("freq")
-    z, place, after, before = ring_neighbours(size)
-    greet(freqs, after, before)
-    copies = start_join(freqs, shrunk, back, sends, recvs, own)
-    copies += start_rows(freqs, picked, pick_timed, psend, precv, pown)
+    there = start_split(freqs, green, gathered, fsend, frecv, fown)
+    ring_gather(size, place, after, whole, arsend, arrecv)
+    fetch.wait()
+    apply_data(data, whole, residual)
+    wr, wi = wave[0], wave[1]
+    re, im = slice(0, picks), slice(picks, both)
+    rr = shots[:, re] - (wr * picked[:, re] - wi * picked[:, im] - residual[:, re])
+    ri = shots[:, im] - (wr * picked[:, im] + wi * picked[:, re] - residual[:, im])
+    residual[:, re] = rr
+    residual[:, im] = ri
+    local[:, re] = wr * rr + wi * ri
+    local[:, im] = wr * ri - wi * rr
+    apply_adjoint(data, residual, adjoint)
+    copies = []
     for step in range(size - 1):
         at = ring_owner((place + 2 * size - 1 - step) % size, size)
         if step:
-            total[step - 1] = held[step - 1] + adjoint[at]
+            total[step - 1] = held[step - 1] + adjoint[part(at), :]
         copy = pltpu.make_async_remote_copy(
-            adjoint.at[at] if step == 0 else total.at[step - 1],
+            adjoint.at[part(at), :] if step == 0 else total.at[step - 1],
             held.at[step], rsend.at[step], rrecv.at[step],
             device_id={"rcv": after}, device_id_type=MESH,
         )
         copy.start()
+        if step == 0:
+            for sent in there:
+                sent.wait()
+            two, count, deep, width = gathered.shape
+            block = pl.BlockSpec((two, count, 8, width), lambda j: (0, 0, j, 0))
+            pltpu.emit_pipeline(
+                lambda x, o: shrink_body(level, keep, x, o),
+                grid=(deep // 8,),
+                in_specs=[block],
+                out_specs=[block],
+            )(gathered, shrunk)
+            copies += start_join(freqs, shrunk, back, sends, recvs, own)
+            copies += start_rows(freqs, picked, pick_timed, psend, precv, pown)
         copy.wait()
-    dir_all[z] = local[...] - (held[size - 2] + adjoint[z])
-    copies += start_rows(freqs, dir_all.at[z], dir_timed, dsend, drecv, down)
+    dir_all[part(z), :] = local[...] - (held[size - 2] + adjoint[part(z), :])
+    copies += start_rows(freqs, dir_all.at[part(z), :], dir_timed, dsend, drecv, down)
     ring_gather(size, place, after, dir_all, gsend, grecv)
+    apply_data(data, dir_all, image)
+    mine = dir_all[part(z), :]
+    gr = wr * mine[:, re] - wi * mine[:, im] - image[:, re]
+    gi = wr * mine[:, im] + wi * mine[:, re] - image[:, im]
+    norms[0] = jnp.full((8, 128), jnp.sum(mine * mine))
+    norms[1] = jnp.full((8, 128), jnp.sum(gr * gr + gi * gi))
     for copy in copies:
         copy.wait()
 
@@ -390,47 +473,45 @@
 DMA = pltpu.SemaphoreType.DMA
 
 
-def first_call(freqs, size, green, picked):
+SMEM = pl.BlockSpec(memory_space=pltpu.SMEM)
+
+
+def first_call(freqs, size, level, wave, green, picked, shots, keep, data):
     two, _, rows, width = green.shape
+    both = picked.shape[1]
+    deep = rows // freqs
+    f32 = jnp.float32
+    split = jax.ShapeDtypeStruct((two, freqs, deep, width), f32)
+    timed = jax.ShapeDtypeStruct((freqs, deep, both), f32)
+    tall = pltpu.VMEM((size * rows, both), f32)
+    flat = pltpu.VMEM((rows, both), f32)
+    trio = [DMA((freqs,)), DMA((freqs,)), DMA(())]
+    ring = [DMA((size,)), DMA((size,))]
     return pl.pallas_call(
         functools.partial(first_body, freqs, size),
         out_shape=(
-            jax.ShapeDtypeStruct((two, freqs, rows // freqs, width), jnp.float32),
-            jax.ShapeDtypeStruct((size,) + picked.shape, jnp.float32),
+            split,
+            split,
+            jax.ShapeDtypeStruct(green.shape, f32),
+            jax.ShapeDtypeStruct(picked.shape, f32),
+            jax.ShapeDtypeStruct((2, 8, 128), f32),
+            timed,
+            timed,
         ),
-        in_specs=[ANY, VMEM],
-        out_specs=(ANY, VMEM),
-        scratch_shapes=[DMA((freqs,)), DMA((freqs,)), DMA(()), DMA((size,)), DMA((size,))],
+        in_specs=[SMEM, SMEM, ANY, VMEM, VMEM, VMEM, ANY],
+        out_specs=(ANY, ANY, ANY, VMEM, VMEM, VMEM, VMEM),
+        scratch_shapes=[
+            tall, tall, tall, flat,
+            pltpu.VMEM((size - 1, rows, both), f32),
+            pltpu.VMEM((size - 2, rows, both), f32),
+            pltpu.VMEM((two, rows, width), f32),
+            flat,
+        ]
+        + trio + trio + ring + ring + ring + trio + trio + [DMA(())],
         compiler_params=pltpu.CompilerParams(
-            collective_id=0, has_side_effects=True, vmem_limit_bytes=40 << 20
+            collective_id=0, has_side_effects=True, vmem_limit_bytes=60 << 20
         ),
-    )(green, picked)
-
-
-def second_call(freqs, size, shrunk, adjoint, local, picked):
-    two, _, part, width = shrunk.shape
-    rows, both = local.shape
-    pair = [DMA((freqs,)), DMA((freqs,)), DMA(())]
-    ring = [DMA((size,)), DMA((size,))]
-    return pl.pallas_call(
-        functools.partial(second_body, freqs, size),
-        out_shape=(
-            jax.ShapeDtypeStruct((two, 1, rows, width), jnp.float32),
-            jax.ShapeDtypeStruct((size, rows, both), jnp.float32),
-            jax.ShapeDtypeStruct((freqs, part, both), jnp.float32),
-            jax.ShapeDtypeStruct((freqs, part, both), jnp.float32),
-        ),
-        in_specs=[ANY, VMEM, VMEM, VMEM],
-        out_specs=(ANY, VMEM, VMEM, VMEM),
-        scratch_shapes=[
-            pltpu.VMEM((size - 1, rows, both), jnp.float32),
-            pltpu.VMEM((size - 2, rows, both), jnp.float32),
-        ]
-        + pair + ring + ring + pair + pair,
-        compiler_params=pltpu.CompilerParams(
-            collective_id=1, has_side_effects=True, vmem_limit_bytes=48 << 20
-        ),
-    )(shrunk, adjoint, local, picked)
+    )(level, wave, green, picked, shots, keep, data)
 
 
 def third_call(freqs, size, level, norms, keep, picks, dirs):
@@ -492,65 +573,58 @@
     freqs = lax.axis_size("freq")
     size = lax.axis_size("rcv")
     fast = rows_here % (8 * freqs) == 0 and size % 2 == 0 and size > 2
+    fast = fast and width % CHUNK == 0 and picks % 128 == 0
     places = jnp.arange(width, dtype=jnp.int32)
     pickcat = pick_call((places[:, None] == sources[None, :]).astype(jnp.bfloat16), green_freq)
     picked = (pickcat[:, :picks], pickcat[:, picks:])
+    keep_cols = jnp.take(keep_all, sources, axis=1)
+    wr = wavelet[0, 0]
+    wi = wavelet[1, 0]
     if fast:
-        gathered, both = first_call(freqs, size, green_freq, pickcat)
-        both = both.reshape(size * rows_here, 2 * picks)
+        wave = wavelet[:, 0]
+        shots = jnp.concatenate([shot_panels[0, 0], shot_panels[1, 0]], axis=1)
+        _, _, back, resid, norms, dir_timed, pick_timed = first_call(
+            freqs, size, threshold, wave, green_freq, pickcat, shots, keep_all, data_matrix
+        )
+        cols_back = third_call(
+            freqs, size, threshold, norms, keep_cols, pick_timed, dir_timed
+        )
+        residual = jnp.stack([resid[:, :picks], resid[:, picks:]])[:, None]
     else:
         gathered = lax.all_to_all(green_freq, "freq", split_axis=2, concat_axis=1, tiled=True)
         both = lax.all_gather(pickcat, "rcv", axis=0, tiled=True)
-    wr = wavelet[0, 0]
-    wi = wavelet[1, 0]
-    dr = data_matrix[0, 0]
-    di = data_matrix[1, 0]
-    flipped = jnp.concatenate([-both[:, picks:], both[:, :picks]], axis=1)
-    multiple = apply_rows(dr, di, both, flipped)
-    resid_real = shot_panels[0, 0] - (wr * picked[0] - wi * picked[1] - multiple[:, :picks])
-    resid_imag = shot_panels[1, 0] - (wr * picked[1] + wi * picked[0] - multiple[:, picks:])
-    residual = jnp.stack([resid_real, resid_imag])[:, None]
-    down = ((0,), (0,))
-    rboth = jnp.concatenate([resid_real, resid_imag], axis=1)
-    rflip = jnp.concatenate([resid_imag, -resid_real], axis=1)
-    adjoint = dots(dr, rboth, down) + dots(di, rflip, down)
-    shrunk = shrink_call(threshold, keep_all, (gathered,))
-    local = jnp.concatenate(
-        [wr * resid_real + wi * resid_imag, wr * resid_imag - wi * resid_real], axis=1
-    )
-    if fast:
-        back, dir_all, dir_timed, pick_timed = second_call(
-            freqs, size, shrunk, adjoint.reshape(size, rows_here, 2 * picks), local, pickcat
-        )
-        direction = lax.dynamic_index_in_dim(dir_all, lax.axis_index("rcv"), 0, keepdims=False)
-        dir_all = dir_all.reshape(size * rows_here, 2 * picks)
-    else:
-        reduced = lax.psum_scatter(adjoint, "rcv", scatter_dimension=0, tiled=True)
-        direction = local - reduced
+        dr = data_matrix[0, 0]
+        di = data_matrix[1, 0]
+        flipped = jnp.concatenate([-both[:, picks:], both[:, :picks]], axis=1)
+        multiple = apply_rows(dr, di, both, flipped)
+        resid_real = shot_panels[0, 0] - (wr * picked[0] - wi * picked[1] - multiple[:, :picks])
+        resid_imag = shot_panels[1, 0] - (wr * picked[1] + wi * picked[0] - multiple[:, picks:])
+        residual = jnp.stack([resid_real, resid_imag])[:, None]
+        down = ((0,), (0,))
+        rboth = jnp.concatenate([resid_real, resid_imag], axis=1)
+        rflip = jnp.concatenate([resid_imag, -resid_real], axis=1)
+        adjoint = dots(dr, rboth, down) + dots(di, rflip, down)
+        local = jnp.concatenate(
+            [wr * resid_real + wi * resid_imag, wr * resid_imag - wi * resid_real], axis=1
+        )
+        direction = local - lax.psum_scatter(adjoint, "rcv", scatter_dimension=0, tiled=True)
         dir_all = lax.all_gather(direction, "rcv", axis=0, tiled=True)
+        shrunk = shrink_call(threshold, keep_all, (gathered,))
         back = lax.all_to_all(shrunk, "freq", split_axis=1, concat_axis=2, tiled=True)
+        dir_real = direction[:, :picks]
+        dir_imag = direction[:, picks:]
         dir_timed = lax.all_to_all(
-            jnp.stack([direction[:, :picks], direction[:, picks:]])[:, None],
+            jnp.stack([dir_real, dir_imag])[:, None],
             "freq", split_axis=2, concat_axis=1, tiled=True,
         )
-    dir_real = direction[:, :picks]
-    dir_imag = direction[:, picks:]
-    pushed = apply_rows(
-        dr, di, dir_all, jnp.concatenate([-dir_all[:, picks:], dir_all[:, :picks]], axis=1)
-    )
-    image_real = wr * dir_real - wi * dir_imag - pushed[:, :picks]
-    image_imag = wr * dir_imag + wi * dir_real - pushed[:, picks:]
-    norm_dir = jnp.sum(direction * direction)
-    norm_img = jnp.sum(image_real * image_real + image_imag * image_imag)
-    keep_cols = jnp.take(keep_all, sources, axis=1)
-    norms = jnp.stack([norm_dir, norm_img])
-    if fast:
-        cols_back = third_call(
-            freqs, size, threshold, jnp.broadcast_to(norms[:, None, None], (2, 8, 128)),
-            keep_cols, pick_timed, dir_timed,
-        )
-    else:
-        totals = lax.psum(norms, ("freq", "rcv"))
+        pushed = apply_rows(
+            dr, di, dir_all, jnp.concatenate([-dir_all[:, picks:], dir_all[:, :picks]], axis=1)
+        )
+        image_real = wr * dir_real - wi * dir_imag - pushed[:, :picks]
+        image_imag = wr * dir_imag + wi * dir_real - pushed[:, picks:]
+        norm_dir = jnp.sum(direction * direction)
+        norm_img = jnp.sum(image_real * image_real + image_imag * image_imag)
+        totals = lax.psum(jnp.stack([norm_dir, norm_img]), ("freq", "rcv"))
         scalars = jnp.concatenate([threshold, (totals[0] / totals[1])[None]])
         pick_timed = jnp.take(gathered, sources, axis=3)
         cols = shrink_call(scalars, keep_cols, (pick_timed, dir_timed))

time: 413 us -> 342 us (0.83)
  matrix products: 32.6 us -> 0 us
  Pallas kernels: 346 us -> 328 us
  other arithmetic: 17.6 us -> 6.21 us
  local copies, waits for them, and re-layouts: 14.7 us -> 5.52 us
    dot_general x6 -> x0, matrix products: 32.6 us -> none  [dots(): return lax.dot_general(lhs, rhs, (contract, ((), ())), precision=HIGH)]
    pallas_call x3 -> x1, Pallas kernels: 298 us -> 278 us  [first_call(): pl.pallas_call(functools.partial(first_body, freqs, size), out_shape=(spl...]
    add x1 -> x0, local copies, waits for them, and re-layouts: 6.09 us -> none  [on_device(): adjoint = dots(dr, rboth, down) + dots(di, rflip, down)]
    reduce_sum x2 -> x0, other arithmetic: 4.21 us -> none  [the longest x1 2.18 us: on_device(): norm_dir = jnp.sum(direction * direction)]
where the time goes in v2:
time: 342 us; the launch traced here: 341 us
  Pallas kernels  328 us (96%)
  other arithmetic  6.21 us (2%)
  local copies, waits for them, and re-layouts  5.52 us (2%)
    pallas_call x1, Pallas kernels, first_call(): pl.pallas_call(functools.partial(first_body, freqs, size), out_shape=(spl...  278 us
    pallas_call x1, Pallas kernels, third_call(): pl.pallas_call(functools.partial(third_body, freqs, size), out_shape=jax....  30.3 us
    pallas_call x1, Pallas kernels, merge_call(): pl.pallas_call(merge_body, grid=(rows // tile,), in_specs=[pl.BlockSpec((...  11.2 us
    pallas_call x1, Pallas kernels, pick_call(): pl.pallas_call(pick_body, grid=(rows // tile,), in_specs=[pl.BlockSpec((w...  8.46 us

profile of v2, /device:TPU:1, one launch (start us, length us, event | category | flops | bytes accessed | tf_op | source)
XLA Modules:
  0.0 341.0 jit_solution(8188738674360991573)
XLA Ops:
  0.6 1.3 slice_bitcast_fusion.3
  2.0 0.0 copy-start.6
  2.0 0.0 copy-start.7
  2.0 1.2 pad_maximum_fusion.shots
  3.2 0.0 copy-done.6
  3.2 0.6 convert_element_type.18.keep
  4.5 0.0 copy-done.7
  4.5 1.6 fusion.2.hot_ref
  6.1 8.5 %shard_map.86.picked = f32[576,512]{1,0:T(8,128)} custom-call(bf16[2304,256]{1,0:T(8,128)(2,1)} %fusion.2.hot_ref, f32[2,1,576,2304]{3,2,1,0:T(8,128)} %green.1), custom_call_target="tpu_custom_call" | custom-call | tf_op jit(solution)/shard_map/pallas_call | solution.py:556
  14.5 0.0 copy-start.5
  14.5 277.9 %shard_map.87 = (f32[2,8,72,2304]{3,2,1,0:T(8,128)}, f32[2,8,72,2304]{3,2,1,0:T(8,128)}, f32[2,1,576,2304]{3,2,1,0:T(8,128)}, f32[576,512]{1,0:T(8,128)}, f32[2,...) custom-call(f32[1]{0:T(128)S(6)} %copy.12.level.level_ref, f32[2]{0:T(128)} %bitcast.15, ...), custom_call_target="tpu_custom_call" | custom-call | tf_op jit(solution)/shard_map/pallas_call | solution.py:490
  292.4 0.0 copy-start.1
  292.4 0.0 copy-start.3
  292.4 0.0 copy-done.5
  292.4 0.4 copy.9
  292.8 0.7 gather_fusion
  293.6 0.1 copy.10
  293.6 0.0 copy-done.1
  293.7 0.0 copy-done.3
  293.7 0.0 copy-start.2
  293.7 1.3 copy-done.2
  294.9 30.3 %shard_map.88.cols_ref = f32[576,512]{1,0:T(8,128)S(1)} custom-call(f32[1]{0:T(128)S(6)} %copy.12.level.level_ref, f32[2,8,128]{2,1,0:T(8,128)S(1)} %copy-done.3, f32[8,256]{1,0:T(8,128)S(1)} %select_bitcast_fusion.keep, f32[8,72,512]{2,1,0:T(8,128)S(1)} %copy-done.2, f32[8,72,512]{2,1,0:T(8,128)S(1)} %copy-done.1), custom_call_target="tpu_custom_call" | custom-call | tf_op jit(solution)/shard_map/pallas_call | solution.py:519
  325.3 0.0 copy-start
  325.3 1.0 copy-done
  326.3 1.6 fusion
  328.0 0.6 reshape.21.mask_ref
  328.6 0.0 copy-start.4
  328.6 11.2 %shard_map.89 = f32[2,1,576,2304]{3,2,1,0:T(8,128)} custom-call(f32[1,2304]{1,0:T(1,128)} %reshape.21.mask_ref, bf16[256,2304]{1,0:T(8,128)(2,1)} %get-tuple-element.18.hot_ref, f32[576,512]{1,0:T(8,128)} %copy-done, f32[2,1,576,2304]{3,2,1,0:T(8,128)} %get-tuple-element.10.back_ref), custom_call_target="tpu_custom_call" | custom-call | tf_op jit(solution)/shard_map/pallas_call | solution.py:136
  339.8 0.0 copy-done.4
  339.8 0.1 slice_bitcast_fusion.1
  339.9 1.1 maximum_bitcast_fusion
  (5 shorter events, 0.0 us)
Async XLA Ops:
  2.0 1.2 copy-start.6
  2.0 2.5 copy-start.7
  14.5 277.9 %copy-start.5 = (f32[8,2304]{1,0:T(8,128)S(1)}, f32[8,2304]{1,0:T(8,128)}, u32[]{:S(2)}) copy-start(f32[8,2304]{1,0:T(8,128)} %convert_element_type.18.keep) | copy-start | bytes 221188
  292.4 1.3 copy-start.1
  292.4 1.3 copy-start.3
  293.7 1.3 copy-start.2
  325.3 1.0 copy-start
  328.6 11.2 %copy-start.4 = (f32[576,512]{1,0:T(8,128)S(1)}, f32[576,512]{1,0:T(8,128)}, u32[]{:S(2)}) copy-start(f32[576,512]{1,0:T(8,128)} %get-tuple-element.11) | copy-start | bytes 3538948
